TPU v7x, 512 devices: a whole 4x4x16 slice. The times are simulated.
512 devices in a mesh: seq: 64 (over z, y), dp: 8 (over x, core).
Axes of the slice: x: 4, y: 4, z: 16, core: 2. Of those that a mesh axis runs over, the one named last changes fastest.
Arguments:
- queries: bfloat16 [8, 8192, 2048], P('dp', 'seq'), may hold values from -40 to 40
- keys: bfloat16 [8, 8192, 2048], P('dp', 'seq'), may hold values from -6 to 6
- values: bfloat16 [8, 8192, 2048], P('dp', 'seq'), may hold values from -6 to 6
- grad_out: bfloat16 [8, 8192, 2048], P('dp', 'seq'), may hold values from -48 to 48
- lengths: int32 [8], P('dp'), may hold values from 1024 to 8192, as said below
- fields: int32 [8, 8192], P('dp', 'seq'), may hold values from 0 to 63
- field_bias: bfloat16 [16, 64], replicated, may hold values from -6 to 6
Outputs:
- grad_queries: bfloat16 [8, 8192, 2048], P('dp', 'seq')
- grad_keys: bfloat16 [8, 8192, 2048], P('dp', 'seq')
- grad_values: bfloat16 [8, 8192, 2048], P('dp', 'seq')
- grad_bias: float32 [16, 64], replicated
Inputs may be any that keep to these rules, and one draw needn't show every extreme that they name: `lengths`: the valid positions of a sequence form a prefix; in every draw some sequence is full.
All inputs are finite; a program needn't handle non-finite values.
Results may differ from a plain program's by a relative error of at most 0.0077.
Values may be sent and summed in bfloat16 or wider, within the bound.
A program may use at most 128 MiB of HBM per device.

v0:
```python
import jax
import jax.numpy as jnp
from jax import lax
from jax.sharding import PartitionSpec as P

HEADS = 16
HEAD_DIM = 128
WINDOW = 512
FIELDS = 64


def passed_along(value, axis, steps):
    count = lax.axis_size(axis)
    first, last = (max(0, -steps), min(count, count - steps))
    return lax.ppermute(value, axis, [(source, source + steps) for source in range(first, last)])


def split_heads(rows):
    return rows.reshape(rows.shape[0], HEADS, HEAD_DIM)


def band_mask(query_places, key_places, length):
    not_after = key_places[None, :] <= query_places[:, None]
    inside = key_places[None, :] > query_places[:, None] - WINDOW
    started = key_places[None, :] >= 0
    live_rows = query_places[:, None] < length
    return not_after & inside & started & live_rows


def logits_of(query_heads, key_heads, key_bias):
    factor = HEAD_DIM ** (-0.5)
    products = jnp.einsum(
        "qhd,khd->hqk", query_heads, key_heads, preferred_element_type=jnp.float32
    )
    return products * factor + key_bias[:, None, :]


def grad_logits_of(attn_weights, row_delta, grad_heads, value_heads):
    grad_probs = jnp.einsum(
        "qhd,khd->hqk", grad_heads, value_heads, preferred_element_type=jnp.float32
    )
    return attn_weights * (grad_probs - row_delta[:, :, None])


def shards(queries, keys, values, grad_out, lengths, fields, field_bias):
    tok_rows = queries.shape[1]
    row_width = queries.shape[2]
    length = lengths[0]
    query_own = queries[0]
    key_own = keys[0]
    value_own = values[0]
    grad_own = grad_out[0]
    reach_blocks = WINDOW // tok_rows
    factor = HEAD_DIM ** (-0.5)
    block_index = lax.axis_index("seq")
    onehot = (fields[0][:, None] == jnp.arange(FIELDS, dtype=jnp.int32)[None, :]).astype(
        jnp.bfloat16
    )
    own_bias = jnp.dot(field_bias, onehot.T, preferred_element_type=jnp.float32).astype(
        jnp.bfloat16
    )
    package = (key_own, value_own, own_bias)
    arrived = []
    for distance in range(1, reach_blocks + 1):
        arrived.append(passed_along((package[0], package[1], package[2]), "seq", distance))
    ordered = arrived[::-1] + [package]
    key_all = jnp.concatenate([arrival[0] for arrival in ordered], axis=0)
    value_all = jnp.concatenate([arrival[1] for arrival in ordered], axis=0)
    bias_all = jnp.concatenate([arrival[2] for arrival in ordered], axis=1).astype(jnp.float32)
    query_places = block_index * tok_rows + jnp.arange(tok_rows, dtype=jnp.int32)
    key_places = (block_index - reach_blocks) * tok_rows + jnp.arange(
        (reach_blocks + 1) * tok_rows, dtype=jnp.int32
    )
    query_heads = split_heads(query_own)
    grad_heads = split_heads(grad_own)
    key_heads = split_heads(key_all)
    value_heads = split_heads(value_all)
    logits = logits_of(query_heads, key_heads, bias_all)
    visible = band_mask(query_places, key_places, length)[None]
    live_rows = (query_places < length)[None, :, None]
    row_peak = jnp.max(jnp.where(visible, logits, -1e30), axis=2, keepdims=True)
    powers = jnp.where(visible, jnp.exp(logits - row_peak), 0.0)
    totals = jnp.where(live_rows, jnp.sum(powers, axis=2, keepdims=True), 1.0)
    attn_weights = powers / totals
    weights_low = attn_weights.astype(jnp.bfloat16)
    outputs = jnp.einsum(
        "hqk,khd->qhd", weights_low, value_heads, preferred_element_type=jnp.float32
    )
    row_delta = jnp.einsum("qhd,qhd->hq", grad_heads.astype(jnp.float32), outputs)
    grad_logits = grad_logits_of(attn_weights, row_delta, grad_heads, value_heads)
    grad_low = grad_logits.astype(jnp.bfloat16)
    grad_query = (
        jnp.einsum("hqk,khd->qhd", grad_low, key_heads, preferred_element_type=jnp.float32) * factor
    )
    own_cols = reach_blocks * tok_rows
    grad_key = (
        jnp.einsum(
            "hqk,qhd->khd", grad_low, query_heads, preferred_element_type=jnp.float32
        ).reshape(-1, row_width)
        * factor
    )
    grad_value = jnp.einsum(
        "hqk,qhd->khd", weights_low, grad_heads, preferred_element_type=jnp.float32
    ).reshape(-1, row_width)
    column = jnp.sum(grad_logits, axis=1)
    key_total = grad_key[own_cols:]
    value_total = grad_value[own_cols:]
    column_total = column[:, own_cols:]
    for distance in range(1, reach_blocks + 1):
        first_row = (reach_blocks - distance) * tok_rows
        returned = passed_along(
            (
                grad_key[first_row : first_row + tok_rows],
                grad_value[first_row : first_row + tok_rows],
                column[:, first_row : first_row + tok_rows],
            ),
            "seq",
            -distance,
        )
        key_total = key_total + returned[0]
        value_total = value_total + returned[1]
        column_total = column_total + returned[2]
    bias_local = jnp.dot(column_total, onehot.astype(jnp.float32), precision=lax.Precision.HIGHEST)
    query_low = grad_query.reshape(tok_rows, row_width).astype(jnp.bfloat16)
    key_low = key_total.astype(jnp.bfloat16)
    value_low = value_total.astype(jnp.bfloat16)
    bias_total = lax.psum(bias_local, ("seq", "dp"))
    return (
        query_low.reshape(1, tok_rows, row_width),
        key_low.reshape(1, tok_rows, row_width),
        value_low.reshape(1, tok_rows, row_width),
        bias_total,
    )


def solution(mesh):
    return jax.shard_map(
        shards,
        mesh=mesh,
        in_specs=(
            P("dp", "seq", None),
            P("dp", "seq", None),
            P("dp", "seq", None),
            P("dp", "seq", None),
            P("dp"),
            P("dp", "seq"),
            P(),
        ),
        out_specs=(P("dp", "seq", None), P("dp", "seq", None), P("dp", "seq", None), P()),
        check_vma=False,
    )
```

profile of v0, /device:TPU:1, one launch (start us, length us, event | category | flops | bytes accessed | tf_op | source)
XLA Modules:
  0.0 491.5 jit_solution(1476968906301964713)
XLA Ops:
  2.2 4.2 collective-permute-start.7
  6.4 4.5 collective-permute-start.6
  12.2 2.6 collective-permute-start.11
  14.9 4.8 collective-permute-start.10
  19.7 4.2 collective-permute-start.9
  24.6 2.6 collective-permute-start.5
  27.3 4.8 collective-permute-start.4
  38.1 5.2 %collective-permute-done.5 = bf16[16,128]{1,0:T(8,128)(2,1)S(1)} collective-permute-done((bf16[16,128]{1,0:T(8,128)(2,1)S(1)}, bf16[16,128]{1,0:T(8,128)(2,1)S(1)}, u32[]{:S(2)}, u32[]{:S(2)}) %collective-permute-start.5) | collective-permute-done | bytes 4128 | tf_op jit(solution)/shard_map/ppermute | solution.py:15
  44.7 18.3 %collective-permute-start.3 = (bf16[128,2048]{0,1:T(8,128)(2,1)S(1)}, bf16[128,2048]{0,1:T(8,128)(2,1)}, u32[]{:S(2)}, u32[]{:S(2)}) collective-permute-start(bf16[128,2048]{0,1:T(8,128)(2,1)S(1)} %bitcast.102), channel_id=1, source_target_pairs={{0,8},{8,16},{16,24},{24,32},{32,40},{40,48},{48,56},{56,64},{64,7... | collective-permute-start | bytes 1572872 | tf_op jit(solution)/shard_map/ppermute | solution.py:15
  63.0 9.7 %collective-permute-start.2 = (bf16[128,2048]{0,1:T(8,128)(2,1)S(1)}, bf16[128,2048]{0,1:T(8,128)(2,1)}, u32[]{:S(2)}, u32[]{:S(2)}) collective-permute-start(bf16[128,2048]{0,1:T(8,128)(2,1)S(1)} %bitcast.103), channel_id=1, source_target_pairs={{0,16},{8,24},{16,32},{24,40},{32,48},{40,56},{48,64},{56,72},{64,... | collective-permute-start | bytes 1572872 | tf_op jit(solution)/shard_map/ppermute | solution.py:15
  72.7 5.3 %collective-permute-start.1 = (bf16[128,2048]{0,1:T(8,128)(2,1)S(1)}, bf16[128,2048]{0,1:T(8,128)(2,1)}, u32[]{:S(2)}, u32[]{:S(2)}) collective-permute-start(bf16[128,2048]{0,1:T(8,128)(2,1)S(1)} %bitcast.104), channel_id=1, source_target_pairs={{0,24},{8,32},{16,40},{24,48},{32,56},{40,64},{48,72},{56,80},{64,... | collective-permute-start | bytes 1572872 | tf_op jit(solution)/shard_map/ppermute | solution.py:15
  78.0 2.1 collective-permute-start
  82.3 2.0 copy.38
  89.5 4.0 collective-permute-done.1
  104.6 7.6 %fusion.34 = (f32[16,128]{1,0:T(8,128)S(1)}, f32[16,128,640]{1,2,0:T(8,128)}) fusion(f32[16,640]{1,0:T(8,128)S(1)} %convert_element_type.46, pred[128,640]{0,1:T(8,128)(4,1)S(1)} %and_and_fusion, bf16[640,16,128]{2,0,1:T(8,128)(2,1)} %constant_dynamic-update-slice_fusion, bf16[128,16,128]{0,2,1:T(8,128)(2,1)} %bitcast.94), kind=kOutput, calls=%fused_computation.67 | convolution fusion | flops 681575040 | bytes 8519680 | tf_op jit(solution)/shard_map/sub | solution.py:82
  117.3 3.3 fusion.8
  122.6 2.6 copy.69
  126.9 5.2 %fusion.35 = (f32[16,640]{1,0:T(8,128)S(1)}, bf16[16,128,640]{1,2,0:T(8,128)(2,1)S(1)}) fusion(f32[16,128]{1,0:T(8,128)S(1)} %copy.70, bf16[640,16,128]{2,0,1:T(8,128)(2,1)} %copy-done.5, bf16[128,16,128]{0,2,1:T(8,128)(2,1)} %copy.55, f32[16,128,640]{1,2,0:T(8,128)} %get-tuple-element.27, f32[16,128]{1,0:T(8,128)S(1)} %broadcast_select_fusion), kind=kOutput, calls=%fused_computation.68 | convolution fusion | flops 342087680 | bytes 11067392 | tf_op jit(solution)/shard_map/qhd,khd->hqk/dot_general | solution.py:39
  133.5 2.4 fusion.32
  135.9 2.5 copy.52
  138.4 2.5 copy.51
  141.0 2.6 copy.50
  150.1 2.6 copy.53
  152.6 15.2 %collective-permute-done.20 = f32[16,128]{1,0:T(8,128)S(1)} collective-permute-done((f32[16,128]{1,0:T(8,128)S(1)}, f32[16,128]{1,0:T(8,128)S(1)}, u32[]{:S(2)}, u32[]{:S(2)}) %collective-permute-start.20) | collective-permute-done | bytes 8224 | tf_op jit(solution)/shard_map/ppermute | solution.py:15
  169.2 109.7 %collective-permute-done.23 = f32[16,128]{1,0:T(8,128)S(1)} collective-permute-done((f32[16,128]{1,0:T(8,128)S(1)}, f32[16,128]{1,0:T(8,128)S(1)}, u32[]{:S(2)}, u32[]{:S(2)}) %collective-permute-start.23) | collective-permute-done | bytes 8224 | tf_op jit(solution)/shard_map/ppermute | solution.py:15
  281.2 2.8 collective-permute-done.22
  290.2 2.7 copy.59
  292.9 2.6 copy.58
  300.7 2.8 fusion.11
  306.6 178.1 %psum.7 = f32[16,64]{1,0:T(8,128)} all-reduce(f32[16,64]{1,0:T(8,128)S(1)} %fusion.22), channel_id=1, replica_groups=mesh['seq'=64,'dp'=8] {'seq','dp'}, use_global_device_ids=true, to_apply=%region_3.4 | all-reduce | flops 1024 | bytes 8192 | tf_op jit(solution)/shard_map/psum | solution.py:127
  484.7 2.4 fusion.18
  488.1 3.4 fusion.19
  (113 shorter events, 64.3 us)
Async XLA Ops:
  0.6 35.0 %copy-start.12 = (bf16[1,128,2048]{2,1,0:T(8,128)(2,1)S(1)}, bf16[1,128,2048]{2,1,0:T(8,128)(2,1)}, u32[]{:S(2)}) copy-start(bf16[1,128,2048]{2,1,0:T(8,128)(2,1)} %param.7) | copy-start | bytes 1572868
  2.2 34.5 %copy-start.13 = (bf16[1,128,2048]{2,1,0:T(8,128)(2,1)S(1)}, bf16[1,128,2048]{2,1,0:T(8,128)(2,1)}, u32[]{:S(2)}) copy-start(bf16[1,128,2048]{2,1,0:T(8,128)(2,1)} %param.10) | copy-start | bytes 1572868
  2.2 22.4 %collective-permute-start.7 = (bf16[16,128]{1,0:T(8,128)(2,1)S(1)}, bf16[16,128]{1,0:T(8,128)(2,1)S(1)}, u32[]{:S(2)}, u32[]{:S(2)}) collective-permute-start(bf16[16,128]{1,0:T(8,128)(2,1)S(1)} %fusion.14), channel_id=1, source_target_pairs={{0,8},{8,16},{16,24},{24,32},{32,40},{40,48},{48,56},{56,64},{64,7... | collective-permute-start | bytes 12296 | tf_op jit(solution)/shard_map/ppermute | solution.py:15
  6.4 20.9 %collective-permute-start.6 = (bf16[16,128]{1,0:T(8,128)(2,1)S(1)}, bf16[16,128]{1,0:T(8,128)(2,1)S(1)}, u32[]{:S(2)}, u32[]{:S(2)}) collective-permute-start(bf16[16,128]{1,0:T(8,128)(2,1)S(1)} %fusion.14), channel_id=1, source_target_pairs={{0,16},{8,24},{16,32},{24,40},{32,48},{40,56},{48,64},{56,72},{64,... | collective-permute-start | bytes 12296 | tf_op jit(solution)/shard_map/ppermute | solution.py:15
  12.2 50.8 %collective-permute-start.11 = (bf16[128,2048]{0,1:T(8,128)(2,1)S(1)}, bf16[128,2048]{0,1:T(8,128)(2,1)S(1)}, u32[]{:S(2)}, u32[]{:S(2)}) collective-permute-start(bf16[128,2048]{0,1:T(8,128)(2,1)S(1)} %bitcast.96), channel_id=1, source_target_pairs={{0,8},{8,16},{16,24},{24,32},{32,40},{40,48},{48,56},{56,64},{64,7... | collective-permute-start | bytes 1572872 | tf_op jit(solution)/shard_map/ppermute | solution.py:15
  14.9 57.8 %collective-permute-start.10 = (bf16[128,2048]{0,1:T(8,128)(2,1)S(1)}, bf16[128,2048]{0,1:T(8,128)(2,1)S(1)}, u32[]{:S(2)}, u32[]{:S(2)}) collective-permute-start(bf16[128,2048]{0,1:T(8,128)(2,1)S(1)} %bitcast.97), channel_id=1, source_target_pairs={{0,16},{8,24},{16,32},{24,40},{32,48},{40,56},{48,64},{56,72},{64,... | collective-permute-start | bytes 1572872 | tf_op jit(solution)/shard_map/ppermute | solution.py:15
  19.7 58.3 %collective-permute-start.9 = (bf16[128,2048]{0,1:T(8,128)(2,1)S(1)}, bf16[128,2048]{0,1:T(8,128)(2,1)}, u32[]{:S(2)}, u32[]{:S(2)}) collective-permute-start(bf16[128,2048]{0,1:T(8,128)(2,1)S(1)} %bitcast.98), channel_id=1, source_target_pairs={{0,24},{8,32},{16,40},{24,48},{32,56},{40,64},{48,72},{56,80},{64,... | collective-permute-start | bytes 1572872 | tf_op jit(solution)/shard_map/ppermute | solution.py:15
  24.6 18.7 %collective-permute-start.5 = (bf16[16,128]{1,0:T(8,128)(2,1)S(1)}, bf16[16,128]{1,0:T(8,128)(2,1)S(1)}, u32[]{:S(2)}, u32[]{:S(2)}) collective-permute-start(bf16[16,128]{1,0:T(8,128)(2,1)S(1)} %fusion.14), channel_id=1, source_target_pairs={{0,24},{8,32},{16,40},{24,48},{32,56},{40,64},{48,72},{56,80},{64,... | collective-permute-start | bytes 12296 | tf_op jit(solution)/shard_map/ppermute | solution.py:15
  27.3 17.4 %collective-permute-start.4 = (bf16[16,128]{1,0:T(8,128)(2,1)S(1)}, bf16[16,128]{1,0:T(8,128)(2,1)S(1)}, u32[]{:S(2)}, u32[]{:S(2)}) collective-permute-start(bf16[16,128]{1,0:T(8,128)(2,1)S(1)} %fusion.14), channel_id=1, source_target_pairs={{0,32},{8,40},{16,48},{24,56},{32,64},{40,72},{48,80},{56,88},{64,... | collective-permute-start | bytes 12296 | tf_op jit(solution)/shard_map/ppermute | solution.py:15
  43.3 41.0 %collective-permute-start.8 = (bf16[128,2048]{0,1:T(8,128)(2,1)S(1)}, bf16[128,2048]{0,1:T(8,128)(2,1)S(1)}, u32[]{:S(2)}, u32[]{:S(2)}) collective-permute-start(bf16[128,2048]{0,1:T(8,128)(2,1)S(1)} %bitcast.100), channel_id=1, source_target_pairs={{0,32},{8,40},{16,48},{24,56},{32,64},{40,72},{48,80},{56,88},{64,... | collective-permute-start | bytes 1572872 | tf_op jit(solution)/shard_map/ppermute | solution.py:15
  44.7 40.7 %collective-permute-start.3 = (bf16[128,2048]{0,1:T(8,128)(2,1)S(1)}, bf16[128,2048]{0,1:T(8,128)(2,1)}, u32[]{:S(2)}, u32[]{:S(2)}) collective-permute-start(bf16[128,2048]{0,1:T(8,128)(2,1)S(1)} %bitcast.102), channel_id=1, source_target_pairs={{0,8},{8,16},{16,24},{24,32},{32,40},{40,48},{48,56},{56,64},{64,7... | collective-permute-start | bytes 1572872 | tf_op jit(solution)/shard_map/ppermute | solution.py:15
  63.0 24.4 %collective-permute-start.2 = (bf16[128,2048]{0,1:T(8,128)(2,1)S(1)}, bf16[128,2048]{0,1:T(8,128)(2,1)}, u32[]{:S(2)}, u32[]{:S(2)}) collective-permute-start(bf16[128,2048]{0,1:T(8,128)(2,1)S(1)} %bitcast.103), channel_id=1, source_target_pairs={{0,16},{8,24},{16,32},{24,40},{32,48},{40,56},{48,64},{56,72},{64,... | collective-permute-start | bytes 1572872 | tf_op jit(solution)/shard_map/ppermute | solution.py:15
  72.7 20.8 %collective-permute-start.1 = (bf16[128,2048]{0,1:T(8,128)(2,1)S(1)}, bf16[128,2048]{0,1:T(8,128)(2,1)}, u32[]{:S(2)}, u32[]{:S(2)}) collective-permute-start(bf16[128,2048]{0,1:T(8,128)(2,1)S(1)} %bitcast.104), channel_id=1, source_target_pairs={{0,24},{8,32},{16,40},{24,48},{32,56},{40,64},{48,72},{56,80},{64,... | collective-permute-start | bytes 1572872 | tf_op jit(solution)/shard_map/ppermute | solution.py:15
  78.0 17.5 %collective-permute-start = (bf16[128,2048]{0,1:T(8,128)(2,1)S(1)}, bf16[128,2048]{0,1:T(8,128)(2,1)}, u32[]{:S(2)}, u32[]{:S(2)}) collective-permute-start(bf16[128,2048]{0,1:T(8,128)(2,1)S(1)} %bitcast.105), channel_id=1, source_target_pairs={{0,32},{8,40},{16,48},{24,56},{32,64},{40,72},{48,80},{56,88},{64,... | collective-permute-start | bytes 1572872 | tf_op jit(solution)/shard_map/ppermute | solution.py:15
  96.9 6.0 %copy-start.11 = (bf16[128,16,128]{2,0,1:T(8,128)(2,1)S(1)}, bf16[128,16,128]{2,0,1:T(8,128)(2,1)}, u32[]{:S(2)}) copy-start(bf16[128,16,128]{2,0,1:T(8,128)(2,1)} %copy.32) | copy-start | bytes 1572868
  96.9 6.9 %copy-start.10 = (bf16[128,16,128]{2,0,1:T(8,128)(2,1)S(1)}, bf16[128,16,128]{2,0,1:T(8,128)(2,1)}, u32[]{:S(2)}) copy-start(bf16[128,16,128]{2,0,1:T(8,128)(2,1)} %copy.33) | copy-start | bytes 1572868
  126.9 5.2 %copy-start.8 = (bf16[1,128,2048]{1,2,0:T(8,128)(2,1)S(1)}, bf16[1,128,2048]{1,2,0:T(8,128)(2,1)}, u32[]{:S(2)}) copy-start(bf16[1,128,2048]{1,2,0:T(8,128)(2,1)} %copy.76) | copy-start | bytes 1572868
  141.0 139.2 %copy-start.7 = (bf16[128,16,128]{0,2,1:T(8,128)(2,1)S(1)}, bf16[128,16,128]{0,2,1:T(8,128)(2,1)}, u32[]{:S(2)}) copy-start(bf16[128,16,128]{0,2,1:T(8,128)(2,1)} %copy.55) | copy-start | bytes 1572868
  143.6 153.2 %collective-permute-start.12 = (f32[128,2048]{0,1:T(8,128)}, f32[128,2048]{0,1:T(8,128)}, u32[]{:S(2)}, u32[]{:S(2)}) collective-permute-start(f32[128,2048]{0,1:T(8,128)} %bitcast.111), channel_id=1, source_target_pairs={{8,0},{16,8},{24,16},{32,24},{40,32},{48,40},{56,48},{64,56},{72,6... | collective-permute-start | bytes 3145736 | tf_op jit(solution)/shard_map/ppermute | solution.py:15
  144.8 153.2 %collective-permute-start.13 = (f32[128,2048]{0,1:T(8,128)}, f32[128,2048]{0,1:T(8,128)}, u32[]{:S(2)}, u32[]{:S(2)}) collective-permute-start(f32[128,2048]{0,1:T(8,128)} %bitcast.110), channel_id=1, source_target_pairs={{16,0},{24,8},{32,16},{40,24},{48,32},{56,40},{64,48},{72,56},{80,... | collective-permute-start | bytes 3145736 | tf_op jit(solution)/shard_map/ppermute | solution.py:15
  146.1 153.2 %collective-permute-start.14 = (f32[128,2048]{0,1:T(8,128)}, f32[128,2048]{0,1:T(8,128)}, u32[]{:S(2)}, u32[]{:S(2)}) collective-permute-start(f32[128,2048]{0,1:T(8,128)} %bitcast.108), channel_id=1, source_target_pairs={{24,0},{32,8},{40,16},{48,24},{56,32},{64,40},{72,48},{80,56},{88,... | collective-permute-start | bytes 3145736 | tf_op jit(solution)/shard_map/ppermute | solution.py:15
  147.5 20.4 %collective-permute-start.20 = (f32[16,128]{1,0:T(8,128)S(1)}, f32[16,128]{1,0:T(8,128)S(1)}, u32[]{:S(2)}, u32[]{:S(2)}) collective-permute-start(f32[16,128]{1,0:T(8,128)S(1)} %get-tuple-element.22), channel_id=1, source_target_pairs={{8,0},{16,8},{24,16},{32,24},{40,32},{48,40},{56,48},{64,56},{72,6... | collective-permute-start | bytes 24584 | tf_op jit(solution)/shard_map/ppermute | solution.py:15
  148.8 130.1 %collective-permute-start.23 = (f32[16,128]{1,0:T(8,128)S(1)}, f32[16,128]{1,0:T(8,128)S(1)}, u32[]{:S(2)}, u32[]{:S(2)}) collective-permute-start(f32[16,128]{1,0:T(8,128)S(1)} %get-tuple-element.23), channel_id=1, source_target_pairs={{32,0},{40,8},{48,16},{56,24},{64,32},{72,40},{80,48},{88,56},{96,... | collective-permute-start | bytes 24584 | tf_op jit(solution)/shard_map/ppermute | solution.py:15
  167.9 116.2 %collective-permute-start.22 = (f32[16,128]{1,0:T(8,128)S(1)}, f32[16,128]{1,0:T(8,128)S(1)}, u32[]{:S(2)}, u32[]{:S(2)}) collective-permute-start(f32[16,128]{1,0:T(8,128)S(1)} %get-tuple-element.24), channel_id=1, source_target_pairs={{24,0},{32,8},{40,16},{48,24},{56,32},{64,40},{72,48},{80,56},{88,... | collective-permute-start | bytes 24584 | tf_op jit(solution)/shard_map/ppermute | solution.py:15
  278.9 205.8 %collective-permute-start.15 = (f32[128,2048]{0,1:T(8,128)}, f32[128,2048]{0,1:T(8,128)}, u32[]{:S(2)}, u32[]{:S(2)}) collective-permute-start(f32[128,2048]{0,1:T(8,128)} %bitcast.109), channel_id=1, source_target_pairs={{32,0},{40,8},{48,16},{56,24},{64,32},{72,40},{80,48},{88,56},{96,... | collective-permute-start | bytes 3145736 | tf_op jit(solution)/shard_map/ppermute | solution.py:15
  284.0 11.4 %collective-permute-start.21 = (f32[16,128]{1,0:T(8,128)S(1)}, f32[16,128]{1,0:T(8,128)S(1)}, u32[]{:S(2)}, u32[]{:S(2)}) collective-permute-start(f32[16,128]{1,0:T(8,128)S(1)} %get-tuple-element.25), channel_id=1, source_target_pairs={{16,0},{24,8},{32,16},{40,24},{48,32},{56,40},{64,48},{72,56},{80,... | collective-permute-start | bytes 24584 | tf_op jit(solution)/shard_map/ppermute | solution.py:15
  290.2 10.5 %copy-start.3 = (bf16[16,128,640]{1,2,0:T(8,128)(2,1)S(1)}, bf16[16,128,640]{1,2,0:T(8,128)(2,1)}, u32[]{:S(2)}) copy-start(bf16[16,128,640]{1,2,0:T(8,128)(2,1)} %copy-done.2) | copy-start | bytes 7864324
  295.5 192.7 %collective-permute-start.17 = (f32[128,2048]{1,0:T(8,128)}, f32[128,2048]{1,0:T(8,128)}, u32[]{:S(2)}, u32[]{:S(2)}) collective-permute-start(f32[128,2048]{1,0:T(8,128)} %copy.58), channel_id=1, source_target_pairs={{16,0},{24,8},{32,16},{40,24},{48,32},{56,40},{64,48},{72,56},{80,... | collective-permute-start | bytes 3145736 | tf_op jit(solution)/shard_map/ppermute | solution.py:15
  296.8 191.4 %collective-permute-start.18 = (f32[128,2048]{1,0:T(8,128)}, f32[128,2048]{1,0:T(8,128)}, u32[]{:S(2)}, u32[]{:S(2)}) collective-permute-start(f32[128,2048]{1,0:T(8,128)} %copy.59), channel_id=1, source_target_pairs={{24,0},{32,8},{40,16},{48,24},{56,32},{64,40},{72,48},{80,56},{88,... | collective-permute-start | bytes 3145736 | tf_op jit(solution)/shard_map/ppermute | solution.py:15
  298.1 190.1 %collective-permute-start.19 = (f32[128,2048]{1,0:T(8,128)}, f32[128,2048]{1,0:T(8,128)}, u32[]{:S(2)}, u32[]{:S(2)}) collective-permute-start(f32[128,2048]{1,0:T(8,128)} %copy.60), channel_id=1, source_target_pairs={{32,0},{40,8},{48,16},{56,24},{64,32},{72,40},{80,48},{88,56},{96,... | collective-permute-start | bytes 3145736 | tf_op jit(solution)/shard_map/ppermute | solution.py:15
  299.4 188.7 %collective-permute-start.16 = (f32[128,2048]{1,0:T(8,128)}, f32[128,2048]{1,0:T(8,128)}, u32[]{:S(2)}, u32[]{:S(2)}) collective-permute-start(f32[128,2048]{1,0:T(8,128)} %copy.56), channel_id=1, source_target_pairs={{8,0},{16,8},{24,16},{32,24},{40,32},{48,40},{56,48},{64,56},{72,6... | collective-permute-start | bytes 3145736 | tf_op jit(solution)/shard_map/ppermute | solution.py:15
  487.1 4.5 copy-start.1
  (7 other events, 16.0 us)
where the time goes:
time: 493 us; the launch traced here: 492 us
  blocking collectives  178 us (36%)
  waiting for transfers between devices  137 us (28%)
  starting transfers between devices  80.2 us (16%)
  local copies, waits for them, and re-layouts  63.1 us (13%)
  matrix products  20.4 us (4%)
  other arithmetic  10.9 us (2%)
    psum x1, blocking collectives, shards(): bias_total = lax.psum(bias_local, ('seq', 'dp'))  178 us
    ppermute x24, waiting for transfers between devices, passed_along(): lax.ppermute(value, axis, [(source, source + steps) for source in range(f...  137 us
    ppermute x24, starting transfers between devices, passed_along(): lax.ppermute(value, axis, [(source, source + steps) for source in range(f...  80.2 us
    unnamed x48, local copies, waits for them, and re-layouts  20.6 us
    slice x4, local copies, waits for them, and re-layouts, shards(): grad_key[first_row:first_row + tok_rows]  10.2 us
    slice x5, local copies, waits for them, and re-layouts, shards(): grad_value[first_row:first_row + tok_rows]  9.92 us
  transfers between devices with their start and end apart: 24, of which 5 were waited for; matrix products, arithmetic and copies ran while one was open for 8% of the time, Pallas kernels for 0%

commit v1 on v0

--- a/solution.py
+++ b/solution.py
@@ -124,7 +124,8 @@
     query_low = grad_query.reshape(tok_rows, row_width).astype(jnp.bfloat16)
     key_low = key_total.astype(jnp.bfloat16)
     value_low = value_total.astype(jnp.bfloat16)
-    bias_total = lax.psum(bias_local, ("seq", "dp"))
+    blocks = lax.all_gather(bias_local, ("seq", "dp"))
+    bias_total = jnp.sum(blocks, axis=0)
     return (
         query_low.reshape(1, tok_rows, row_width),
         key_low.reshape(1, tok_rows, row_width),

time: 493 us -> 454 us (0.921)
  the two profiles are of different devices: /device:TPU:1 before, /device:TPU:442 now
where the time goes in v1:
time: 454 us; the launch traced here: 452 us
  waiting for transfers between devices  229 us (50%)
  starting transfers between devices  107 us (24%)
  local copies, waits for them, and re-layouts  62.6 us (14%)
  matrix products  24 us (5%)
  between operations  15.3 us (3%)
  other arithmetic  14.3 us (3%)
    ppermute x24, waiting for transfers between devices, passed_along(): lax.ppermute(value, axis, [(source, source + steps) for source in range(f...  229 us
    ppermute x24, starting transfers between devices, passed_along(): lax.ppermute(value, axis, [(source, source + steps) for source in range(f...  107 us
    unnamed x46, local copies, waits for them, and re-layouts  20.1 us
    slice x4, local copies, waits for them, and re-layouts, shards(): grad_key[first_row:first_row + tok_rows]  10.3 us
    slice x5, local copies, waits for them, and re-layouts, shards(): grad_value[first_row:first_row + tok_rows]  9.92 us
    concatenate x6, local copies, waits for them, and re-layouts, shards(): key_all = jnp.concatenate([arrival[0] for arrival in ordered], axis=0)  9.37 us
  transfers between devices with their start and end apart: 25, of which 9 were waited for; matrix products, arithmetic and copies ran while one was open for 13% of the time, Pallas kernels for 0%

profile of v1, /device:TPU:442, one launch (start us, length us, event | category | flops | bytes accessed | tf_op | source)
XLA Modules:
  0.0 452.4 jit_solution(2023028653008071256)
XLA Ops:
  8.7 2.7 collective-permute-start.7
  11.5 4.5 collective-permute-start.6
  17.3 3.8 collective-permute-start.11
  23.5 2.8 collective-permute-start.9
  36.8 31.0 %collective-permute-done.5 = bf16[16,128]{1,0:T(8,128)(2,1)S(1)} collective-permute-done((bf16[16,128]{1,0:T(8,128)(2,1)S(1)}, bf16[16,128]{1,0:T(8,128)(2,1)S(1)}, u32[]{:S(2)}, u32[]{:S(2)}) %collective-permute-start.5) | collective-permute-done | bytes 4128 | tf_op jit(solution)/shard_map/ppermute | solution.py:15
  67.8 2.9 collective-permute-start.8
  72.7 7.4 %collective-permute-start.2 = (bf16[128,2048]{0,1:T(8,128)(2,1)S(1)}, bf16[128,2048]{0,1:T(8,128)(2,1)}, u32[]{:S(2)}, u32[]{:S(2)}) collective-permute-start(bf16[128,2048]{0,1:T(8,128)(2,1)S(1)} %bitcast.105), channel_id=1, source_target_pairs={{0,16},{8,24},{16,32},{24,40},{32,48},{40,56},{48,64},{56,72},{64,... | collective-permute-start | bytes 1572872 | tf_op jit(solution)/shard_map/ppermute | solution.py:15
  89.2 10.4 %collective-permute-done.3 = bf16[128,2048]{0,1:T(8,128)(2,1)} collective-permute-done((bf16[128,2048]{0,1:T(8,128)(2,1)S(1)}, bf16[128,2048]{0,1:T(8,128)(2,1)}, u32[]{:S(2)}, u32[]{:S(2)}) %collective-permute-start.3) | collective-permute-done | bytes 524320 | tf_op jit(solution)/shard_map/ppermute | solution.py:15
  101.7 13.2 %collective-permute-done.2 = bf16[128,2048]{0,1:T(8,128)(2,1)} collective-permute-done((bf16[128,2048]{0,1:T(8,128)(2,1)S(1)}, bf16[128,2048]{0,1:T(8,128)(2,1)}, u32[]{:S(2)}, u32[]{:S(2)}) %collective-permute-start.2) | collective-permute-done | bytes 524320 | tf_op jit(solution)/shard_map/ppermute | solution.py:15
  116.9 9.2 %collective-permute-done.1 = bf16[128,2048]{0,1:T(8,128)(2,1)} collective-permute-done((bf16[128,2048]{0,1:T(8,128)(2,1)S(1)}, bf16[128,2048]{0,1:T(8,128)(2,1)}, u32[]{:S(2)}, u32[]{:S(2)}) %collective-permute-start.1) | collective-permute-done | bytes 524320 | tf_op jit(solution)/shard_map/ppermute | solution.py:15
  128.1 8.0 %collective-permute-done = bf16[128,2048]{0,1:T(8,128)(2,1)} collective-permute-done((bf16[128,2048]{0,1:T(8,128)(2,1)S(1)}, bf16[128,2048]{0,1:T(8,128)(2,1)}, u32[]{:S(2)}, u32[]{:S(2)}) %collective-permute-start) | collective-permute-done | bytes 524320 | tf_op jit(solution)/shard_map/ppermute | solution.py:15
  145.4 7.4 %fusion.34 = (f32[16,128]{1,0:T(8,128)S(1)}, f32[16,128,640]{1,2,0:T(8,128)}) fusion(f32[16,640]{1,0:T(8,128)S(1)} %convert_element_type.46, pred[128,640]{0,1:T(8,128)(4,1)S(1)} %and_and_fusion, bf16[640,16,128]{2,0,1:T(8,128)(2,1)} %constant_dynamic-update-slice_fusion, bf16[128,16,128]{0,2,1:T(8,128)(2,1)} %bitcast.96), kind=kOutput, calls=%fused_computation.67 | convolution fusion | flops 681575040 | bytes 8519680 | tf_op jit(solution)/shard_map/sub | solution.py:82
  157.9 3.3 fusion.8
  163.2 2.6 copy.69
  167.4 6.5 %fusion.35 = (f32[16,640]{1,0:T(8,128)S(1)}, bf16[16,128,640]{1,2,0:T(8,128)(2,1)}) fusion(f32[16,128]{1,0:T(8,128)S(1)} %copy.70, bf16[640,16,128]{2,0,1:T(8,128)(2,1)} %copy-done.4, bf16[128,16,128]{0,2,1:T(8,128)(2,1)} %copy.55, f32[16,128,640]{1,2,0:T(8,128)} %get-tuple-element.27, f32[16,128]{1,0:T(8,128)S(1)} %broadcast_select_fusion), kind=kOutput, calls=%fused_computation.68 | convolution fusion | flops 342087680 | bytes 11067392 | tf_op jit(solution)/shard_map/qhd,khd->hqk/dot_general | solution.py:39
  178.4 7.0 %collective-permute-start.22 = (f32[16,128]{1,0:T(8,128)S(1)}, f32[16,128]{1,0:T(8,128)S(1)}, u32[]{:S(2)}, u32[]{:S(2)}) collective-permute-start(f32[16,128]{1,0:T(8,128)S(1)} %get-tuple-element.24), channel_id=1, source_target_pairs={{24,0},{32,8},{40,16},{48,24},{56,32},{64,40},{72,48},{80,56},{88,... | collective-permute-start | bytes 24584 | tf_op jit(solution)/shard_map/ppermute | solution.py:15
  187.6 5.8 %collective-permute-done.21 = f32[16,128]{1,0:T(8,128)S(1)} collective-permute-done((f32[16,128]{1,0:T(8,128)S(1)}, f32[16,128]{1,0:T(8,128)S(1)}, u32[]{:S(2)}, u32[]{:S(2)}) %collective-permute-start.21) | collective-permute-done | bytes 8224 | tf_op jit(solution)/shard_map/ppermute | solution.py:15
  194.3 2.6 multiply_bitcast_fusion
  204.4 2.6 copy.50
  211.5 5.1 %collective-permute-start.14 = (f32[128,2048]{0,1:T(8,128)}, f32[128,2048]{0,1:T(8,128)}, u32[]{:S(2)}, u32[]{:S(2)}) collective-permute-start(f32[128,2048]{0,1:T(8,128)} %bitcast.111), channel_id=1, source_target_pairs={{24,0},{32,8},{40,16},{48,24},{56,32},{64,40},{72,48},{80,56},{88,... | collective-permute-start | bytes 3145736 | tf_op jit(solution)/shard_map/ppermute | solution.py:15
  216.6 2.6 copy.53
  219.2 4.1 collective-permute-start.15
  229.1 2.7 copy.59
  234.3 4.3 collective-permute-start.17
  238.6 16.7 %collective-permute-done.12 = f32[128,2048]{0,1:T(8,128)} collective-permute-done((f32[128,2048]{0,1:T(8,128)}, f32[128,2048]{0,1:T(8,128)}, u32[]{:S(2)}, u32[]{:S(2)}) %collective-permute-start.12) | collective-permute-done | bytes 1048608 | tf_op jit(solution)/shard_map/ppermute | solution.py:15
  257.2 2.7 collective-permute-start.19
  259.9 35.1 %collective-permute-start.16 = (f32[128,2048]{1,0:T(8,128)}, f32[128,2048]{1,0:T(8,128)}, u32[]{:S(2)}, u32[]{:S(2)}) collective-permute-start(f32[128,2048]{1,0:T(8,128)} %copy.56), channel_id=1, source_target_pairs={{8,0},{16,8},{24,16},{32,24},{40,32},{48,40},{56,48},{64,56},{72,6... | collective-permute-start | bytes 3145736 | tf_op jit(solution)/shard_map/ppermute | solution.py:15
  295.1 2.8 fusion.11
  304.2 32.6 %collective-permute-done.17 = f32[128,2048]{1,0:T(8,128)} collective-permute-done((f32[128,2048]{1,0:T(8,128)}, f32[128,2048]{1,0:T(8,128)}, u32[]{:S(2)}, u32[]{:S(2)}) %collective-permute-start.17) | collective-permute-done | bytes 1048608 | tf_op jit(solution)/shard_map/ppermute | solution.py:15
  336.8 102.0 %collective-permute-done.16 = f32[128,2048]{1,0:T(8,128)} collective-permute-done((f32[128,2048]{1,0:T(8,128)}, f32[128,2048]{1,0:T(8,128)}, u32[]{:S(2)}, u32[]{:S(2)}) %collective-permute-start.16) | collective-permute-done | bytes 1048608 | tf_op jit(solution)/shard_map/ppermute | solution.py:15
  438.8 3.4 fusion.19
  442.2 3.3 reduce_sum.29
  (114 shorter events, 86.0 us)
Async XLA Ops:
  7.2 27.3 %copy-start.11 = (bf16[1,128,2048]{2,1,0:T(8,128)(2,1)S(1)}, bf16[1,128,2048]{2,1,0:T(8,128)(2,1)}, u32[]{:S(2)}) copy-start(bf16[1,128,2048]{2,1,0:T(8,128)(2,1)} %param.7) | copy-start | bytes 1572868
  7.2 435.0 %all-gather.3.cloned.1.call-start = ((), (), s32[]{:S(2)}) async-start(), calls=%async_computation | async-start | bytes 4202496 | tf_op jit(solution)/shard_map/all_gather | solution.py:127
  8.7 26.7 %copy-start.12 = (bf16[1,128,2048]{2,1,0:T(8,128)(2,1)S(1)}, bf16[1,128,2048]{2,1,0:T(8,128)(2,1)}, u32[]{:S(2)}) copy-start(bf16[1,128,2048]{2,1,0:T(8,128)(2,1)} %param.10) | copy-start | bytes 1572868
  8.7 18.2 %collective-permute-start.7 = (bf16[16,128]{1,0:T(8,128)(2,1)S(1)}, bf16[16,128]{1,0:T(8,128)(2,1)S(1)}, u32[]{:S(2)}, u32[]{:S(2)}) collective-permute-start(bf16[16,128]{1,0:T(8,128)(2,1)S(1)} %fusion.14), channel_id=1, source_target_pairs={{0,8},{8,16},{16,24},{24,32},{32,40},{40,48},{48,56},{56,64},{64,7... | collective-permute-start | bytes 12296 | tf_op jit(solution)/shard_map/ppermute | solution.py:15
  11.5 17.4 %collective-permute-start.6 = (bf16[16,128]{1,0:T(8,128)(2,1)S(1)}, bf16[16,128]{1,0:T(8,128)(2,1)S(1)}, u32[]{:S(2)}, u32[]{:S(2)}) collective-permute-start(bf16[16,128]{1,0:T(8,128)(2,1)S(1)} %fusion.14), channel_id=1, source_target_pairs={{0,16},{8,24},{16,32},{24,40},{32,48},{40,56},{48,64},{56,72},{64,... | collective-permute-start | bytes 12296 | tf_op jit(solution)/shard_map/ppermute | solution.py:15
  17.3 55.4 %collective-permute-start.11 = (bf16[128,2048]{0,1:T(8,128)(2,1)S(1)}, bf16[128,2048]{0,1:T(8,128)(2,1)S(1)}, u32[]{:S(2)}, u32[]{:S(2)}) collective-permute-start(bf16[128,2048]{0,1:T(8,128)(2,1)S(1)} %bitcast.98), channel_id=1, source_target_pairs={{0,8},{8,16},{16,24},{24,32},{32,40},{40,48},{48,56},{56,64},{64,7... | collective-permute-start | bytes 1572872 | tf_op jit(solution)/shard_map/ppermute | solution.py:15
  21.1 59.0 %collective-permute-start.10 = (bf16[128,2048]{0,1:T(8,128)(2,1)S(1)}, bf16[128,2048]{0,1:T(8,128)(2,1)S(1)}, u32[]{:S(2)}, u32[]{:S(2)}) collective-permute-start(bf16[128,2048]{0,1:T(8,128)(2,1)S(1)} %bitcast.99), channel_id=1, source_target_pairs={{0,16},{8,24},{16,32},{24,40},{32,48},{40,56},{48,64},{56,72},{64,... | collective-permute-start | bytes 1572872 | tf_op jit(solution)/shard_map/ppermute | solution.py:15
  23.5 58.6 %collective-permute-start.9 = (bf16[128,2048]{0,1:T(8,128)(2,1)S(1)}, bf16[128,2048]{0,1:T(8,128)(2,1)}, u32[]{:S(2)}, u32[]{:S(2)}) collective-permute-start(bf16[128,2048]{0,1:T(8,128)(2,1)S(1)} %bitcast.100), channel_id=1, source_target_pairs={{0,24},{8,32},{16,40},{24,48},{32,56},{40,64},{48,72},{56,80},{64,... | collective-permute-start | bytes 1572872 | tf_op jit(solution)/shard_map/ppermute | solution.py:15
  27.0 40.8 %collective-permute-start.5 = (bf16[16,128]{1,0:T(8,128)(2,1)S(1)}, bf16[16,128]{1,0:T(8,128)(2,1)S(1)}, u32[]{:S(2)}, u32[]{:S(2)}) collective-permute-start(bf16[16,128]{1,0:T(8,128)(2,1)S(1)} %fusion.14), channel_id=1, source_target_pairs={{0,24},{8,32},{16,40},{24,48},{32,56},{40,64},{48,72},{56,80},{64,... | collective-permute-start | bytes 12296 | tf_op jit(solution)/shard_map/ppermute | solution.py:15
  28.9 41.8 %collective-permute-start.4 = (bf16[16,128]{1,0:T(8,128)(2,1)S(1)}, bf16[16,128]{1,0:T(8,128)(2,1)S(1)}, u32[]{:S(2)}, u32[]{:S(2)}) collective-permute-start(bf16[16,128]{1,0:T(8,128)(2,1)S(1)} %fusion.14), channel_id=1, source_target_pairs={{0,32},{8,40},{16,48},{24,56},{32,64},{40,72},{48,80},{56,88},{64,... | collective-permute-start | bytes 12296 | tf_op jit(solution)/shard_map/ppermute | solution.py:15
  67.8 20.4 %collective-permute-start.8 = (bf16[128,2048]{0,1:T(8,128)(2,1)S(1)}, bf16[128,2048]{0,1:T(8,128)(2,1)S(1)}, u32[]{:S(2)}, u32[]{:S(2)}) collective-permute-start(bf16[128,2048]{0,1:T(8,128)(2,1)S(1)} %bitcast.102), channel_id=1, source_target_pairs={{0,32},{8,40},{16,48},{24,56},{32,64},{40,72},{48,80},{56,88},{64,... | collective-permute-start | bytes 1572872 | tf_op jit(solution)/shard_map/ppermute | solution.py:15
  70.7 28.9 %collective-permute-start.3 = (bf16[128,2048]{0,1:T(8,128)(2,1)S(1)}, bf16[128,2048]{0,1:T(8,128)(2,1)}, u32[]{:S(2)}, u32[]{:S(2)}) collective-permute-start(bf16[128,2048]{0,1:T(8,128)(2,1)S(1)} %bitcast.104), channel_id=1, source_target_pairs={{0,8},{8,16},{16,24},{24,32},{32,40},{40,48},{48,56},{56,64},{64,7... | collective-permute-start | bytes 1572872 | tf_op jit(solution)/shard_map/ppermute | solution.py:15
  72.7 42.2 %collective-permute-start.2 = (bf16[128,2048]{0,1:T(8,128)(2,1)S(1)}, bf16[128,2048]{0,1:T(8,128)(2,1)}, u32[]{:S(2)}, u32[]{:S(2)}) collective-permute-start(bf16[128,2048]{0,1:T(8,128)(2,1)S(1)} %bitcast.105), channel_id=1, source_target_pairs={{0,16},{8,24},{16,32},{24,40},{32,48},{40,56},{48,64},{56,72},{64,... | collective-permute-start | bytes 1572872 | tf_op jit(solution)/shard_map/ppermute | solution.py:15
  80.1 46.0 %collective-permute-start.1 = (bf16[128,2048]{0,1:T(8,128)(2,1)S(1)}, bf16[128,2048]{0,1:T(8,128)(2,1)}, u32[]{:S(2)}, u32[]{:S(2)}) collective-permute-start(bf16[128,2048]{0,1:T(8,128)(2,1)S(1)} %bitcast.106), channel_id=1, source_target_pairs={{0,24},{8,32},{16,40},{24,48},{32,56},{40,64},{48,72},{56,80},{64,... | collective-permute-start | bytes 1572872 | tf_op jit(solution)/shard_map/ppermute | solution.py:15
  82.1 54.1 %collective-permute-start = (bf16[128,2048]{0,1:T(8,128)(2,1)S(1)}, bf16[128,2048]{0,1:T(8,128)(2,1)}, u32[]{:S(2)}, u32[]{:S(2)}) collective-permute-start(bf16[128,2048]{0,1:T(8,128)(2,1)S(1)} %bitcast.107), channel_id=1, source_target_pairs={{0,32},{8,40},{16,48},{24,56},{32,64},{40,72},{48,80},{56,88},{64,... | collective-permute-start | bytes 1572872 | tf_op jit(solution)/shard_map/ppermute | solution.py:15
  137.5 7.0 %copy-start.9 = (bf16[128,16,128]{2,0,1:T(8,128)(2,1)S(1)}, bf16[128,16,128]{2,0,1:T(8,128)(2,1)}, u32[]{:S(2)}) copy-start(bf16[128,16,128]{2,0,1:T(8,128)(2,1)} %copy.33) | copy-start | bytes 1572868
  167.4 26.0 %copy-start.13 = (s32[1,128]{1,0:T(1,128)S(1)}, s32[1,128]{1,0:T(1,128)}, u32[]{:S(2)}) copy-start(s32[1,128]{1,0:T(1,128)} %param.12) | copy-start | bytes 1540
  167.4 26.8 %copy-start.7 = (bf16[1,128,2048]{1,2,0:T(8,128)(2,1)S(1)}, bf16[1,128,2048]{1,2,0:T(8,128)(2,1)}, u32[]{:S(2)}) copy-start(bf16[1,128,2048]{1,2,0:T(8,128)(2,1)} %copy.76) | copy-start | bytes 1572868
  173.9 13.6 %collective-permute-start.20 = (f32[16,128]{1,0:T(8,128)S(1)}, f32[16,128]{1,0:T(8,128)S(1)}, u32[]{:S(2)}, u32[]{:S(2)}) collective-permute-start(f32[16,128]{1,0:T(8,128)S(1)} %get-tuple-element.22), channel_id=1, source_target_pairs={{8,0},{16,8},{24,16},{32,24},{40,32},{48,40},{56,48},{64,56},{72,6... | collective-permute-start | bytes 24584 | tf_op jit(solution)/shard_map/ppermute | solution.py:15
  175.8 11.7 %collective-permute-start.23 = (f32[16,128]{1,0:T(8,128)S(1)}, f32[16,128]{1,0:T(8,128)S(1)}, u32[]{:S(2)}, u32[]{:S(2)}) collective-permute-start(f32[16,128]{1,0:T(8,128)S(1)} %get-tuple-element.23), channel_id=1, source_target_pairs={{32,0},{40,8},{48,16},{56,24},{64,32},{72,40},{80,48},{88,56},{96,... | collective-permute-start | bytes 24584 | tf_op jit(solution)/shard_map/ppermute | solution.py:15
  178.4 9.2 %collective-permute-start.22 = (f32[16,128]{1,0:T(8,128)S(1)}, f32[16,128]{1,0:T(8,128)S(1)}, u32[]{:S(2)}, u32[]{:S(2)}) collective-permute-start(f32[16,128]{1,0:T(8,128)S(1)} %get-tuple-element.24), channel_id=1, source_target_pairs={{24,0},{32,8},{40,16},{48,24},{56,32},{64,40},{72,48},{80,56},{88,... | collective-permute-start | bytes 24584 | tf_op jit(solution)/shard_map/ppermute | solution.py:15
  185.4 7.9 %collective-permute-start.21 = (f32[16,128]{1,0:T(8,128)S(1)}, f32[16,128]{1,0:T(8,128)S(1)}, u32[]{:S(2)}, u32[]{:S(2)}) collective-permute-start(f32[16,128]{1,0:T(8,128)S(1)} %get-tuple-element.25), channel_id=1, source_target_pairs={{16,0},{24,8},{32,16},{40,24},{48,32},{56,40},{64,48},{72,56},{80,... | collective-permute-start | bytes 24584 | tf_op jit(solution)/shard_map/ppermute | solution.py:15
  204.4 18.9 %copy-start.6 = (bf16[128,16,128]{0,2,1:T(8,128)(2,1)S(1)}, bf16[128,16,128]{0,2,1:T(8,128)(2,1)}, u32[]{:S(2)}) copy-start(bf16[128,16,128]{0,2,1:T(8,128)(2,1)} %copy.55) | copy-start | bytes 1572868
  207.1 48.2 %collective-permute-start.12 = (f32[128,2048]{0,1:T(8,128)}, f32[128,2048]{0,1:T(8,128)}, u32[]{:S(2)}, u32[]{:S(2)}) collective-permute-start(f32[128,2048]{0,1:T(8,128)} %bitcast.113), channel_id=1, source_target_pairs={{8,0},{16,8},{24,16},{32,24},{40,32},{48,40},{56,48},{64,56},{72,6... | collective-permute-start | bytes 3145736 | tf_op jit(solution)/shard_map/ppermute | solution.py:15
  209.0 48.2 %collective-permute-start.13 = (f32[128,2048]{0,1:T(8,128)}, f32[128,2048]{0,1:T(8,128)}, u32[]{:S(2)}, u32[]{:S(2)}) collective-permute-start(f32[128,2048]{0,1:T(8,128)} %bitcast.112), channel_id=1, source_target_pairs={{16,0},{24,8},{32,16},{40,24},{48,32},{56,40},{64,48},{72,56},{80,... | collective-permute-start | bytes 3145736 | tf_op jit(solution)/shard_map/ppermute | solution.py:15
  211.5 48.4 %collective-permute-start.14 = (f32[128,2048]{0,1:T(8,128)}, f32[128,2048]{0,1:T(8,128)}, u32[]{:S(2)}, u32[]{:S(2)}) collective-permute-start(f32[128,2048]{0,1:T(8,128)} %bitcast.111), channel_id=1, source_target_pairs={{24,0},{32,8},{40,16},{48,24},{56,32},{64,40},{72,48},{80,56},{88,... | collective-permute-start | bytes 3145736 | tf_op jit(solution)/shard_map/ppermute | solution.py:15
  219.2 81.6 %collective-permute-start.15 = (f32[128,2048]{0,1:T(8,128)}, f32[128,2048]{0,1:T(8,128)}, u32[]{:S(2)}, u32[]{:S(2)}) collective-permute-start(f32[128,2048]{0,1:T(8,128)} %bitcast.110), channel_id=1, source_target_pairs={{32,0},{40,8},{48,16},{56,24},{64,32},{72,40},{80,48},{88,56},{96,... | collective-permute-start | bytes 3145736 | tf_op jit(solution)/shard_map/ppermute | solution.py:15
  229.1 66.0 %copy-start.2 = (bf16[16,128,640]{1,2,0:T(8,128)(2,1)S(1)}, bf16[16,128,640]{1,2,0:T(8,128)(2,1)}, u32[]{:S(2)}) copy-start(bf16[16,128,640]{1,2,0:T(8,128)(2,1)} %get-tuple-element.29) | copy-start | bytes 7864324
  234.3 102.4 %collective-permute-start.17 = (f32[128,2048]{1,0:T(8,128)}, f32[128,2048]{1,0:T(8,128)}, u32[]{:S(2)}, u32[]{:S(2)}) collective-permute-start(f32[128,2048]{1,0:T(8,128)} %copy.58), channel_id=1, source_target_pairs={{16,0},{24,8},{32,16},{40,24},{48,32},{56,40},{64,48},{72,56},{80,... | collective-permute-start | bytes 3145736 | tf_op jit(solution)/shard_map/ppermute | solution.py:15
  255.2 81.5 %collective-permute-start.18 = (f32[128,2048]{1,0:T(8,128)}, f32[128,2048]{1,0:T(8,128)}, u32[]{:S(2)}, u32[]{:S(2)}) collective-permute-start(f32[128,2048]{1,0:T(8,128)} %copy.59), channel_id=1, source_target_pairs={{24,0},{32,8},{40,16},{48,24},{56,32},{64,40},{72,48},{80,56},{88,... | collective-permute-start | bytes 3145736 | tf_op jit(solution)/shard_map/ppermute | solution.py:15
  257.2 79.6 %collective-permute-start.19 = (f32[128,2048]{1,0:T(8,128)}, f32[128,2048]{1,0:T(8,128)}, u32[]{:S(2)}, u32[]{:S(2)}) collective-permute-start(f32[128,2048]{1,0:T(8,128)} %copy.60), channel_id=1, source_target_pairs={{32,0},{40,8},{48,16},{56,24},{64,32},{72,40},{80,48},{88,56},{96,... | collective-permute-start | bytes 3145736 | tf_op jit(solution)/shard_map/ppermute | solution.py:15
  259.9 178.9 %collective-permute-start.16 = (f32[128,2048]{1,0:T(8,128)}, f32[128,2048]{1,0:T(8,128)}, u32[]{:S(2)}, u32[]{:S(2)}) collective-permute-start(f32[128,2048]{1,0:T(8,128)} %copy.56), channel_id=1, source_target_pairs={{8,0},{16,8},{24,16},{32,24},{40,32},{48,40},{56,48},{64,56},{72,6... | collective-permute-start | bytes 3145736 | tf_op jit(solution)/shard_map/ppermute | solution.py:15
  (7 other events, 24.5 us)
Sparse Core Ops, SparseCore 0:
  194.4 216.3 all-gather.2
